TPU v7x, 128 devices: a whole 4x4x4 slice. The times are simulated.
128 devices in a mesh: dp: 8 (over x_hi, z), fsdp: 8 (over y, core), enc: 2 (over x_lo).
Axes of the slice: x: 4 (x_hi: 2, x_lo: 2; x = x_hi * 2 + x_lo), y: 4, z: 4, core: 2. Of those that a mesh axis runs over, the one named last changes fastest.
Arguments:
- queries: bfloat16 [12288, 4096], P(('dp', 'fsdp'), 'enc'), may hold values from -9 to 9
- nbr_keys: bfloat16 [384, 128, 4096], P('dp', 'fsdp', 'enc'), may hold values from -6 to 6
- nbr_values: bfloat16 [384, 128, 4096], P('dp', 'fsdp', 'enc'), may hold values from -6 to 6
- out_proj: bfloat16 [4096, 8192], P('enc', 'fsdp'), may hold values from -0.09375 to 0.09375
- nbr_source: int32 [192, 2], replicated, may hold values from 0 to 7, as said below
- nbr_index: int32 [192, 2], replicated, may hold values from 0 to 47
- nbr_count: int32 [192], replicated, may hold values from 1 to 2
- cotangent: bfloat16 [12288, 8192], P('dp', 'fsdp'), may hold values from -2.390625 to 2.390625
Outputs:
- attended: bfloat16 [12288, 4096], P(('dp', 'fsdp'), 'enc')
- grad_queries: bfloat16 [12288, 4096], P(('dp', 'fsdp'), 'enc')
- grad_keys: bfloat16 [384, 128, 4096], P('dp', 'fsdp', 'enc')
- grad_values: bfloat16 [384, 128, 4096], P('dp', 'fsdp', 'enc')
- grad_proj: bfloat16 [4096, 8192], P('enc', 'fsdp')
Inputs may be any that keep to these rules, and one draw needn't show every extreme that they name: `nbr_source`: among the 6 slots of the spans of one device, no source group is named more than 1 times, and some group exactly 1 times.
All inputs are finite; a program needn't handle non-finite values.
Results may differ from a plain program's by a relative error of at most 0.013.
Values may be sent and summed in bfloat16 or wider, within the bound.
A program may use at most 128 MiB of HBM per device.

v0:
```python
import math
import jax
import jax.numpy as jnp
from jax import lax
from jax.sharding import PartitionSpec as P

HEAD_DIM = 128
SPAN = 64
SLOTS = 2


def local(queries, nbr_keys, nbr_values, out_proj, nbr_source, nbr_index, nbr_count, cotangent):
    dp_count = lax.axis_size("dp")
    fsdp_count = lax.axis_size("fsdp")
    peer_count = dp_count * fsdp_count
    token_rows, width_halved = queries.shape
    heads_here = width_halved // HEAD_DIM
    spans_here = token_rows // SPAN
    slot_count = SLOTS * spans_here
    capacity = (slot_count + dp_count - 1) // dp_count
    group_size, piece_rows, piece_width = nbr_keys.shape
    neighbour_len = piece_rows * fsdp_count
    scale = 1.0 / math.sqrt(HEAD_DIM)
    my_group = lax.axis_index("dp")
    my_place = my_group * fsdp_count + lax.axis_index("fsdp")
    all_sources = nbr_source.reshape(peer_count, slot_count)
    all_indices = nbr_index.reshape(peer_count, slot_count)
    slot_iota = jnp.arange(slot_count, dtype=jnp.int32)
    earlier = slot_iota[None, :] < slot_iota[:, None]
    same_source = all_sources[:, :, None] == all_sources[:, None, :]
    ranks = jnp.sum(jnp.logical_and(same_source, earlier[None]), axis=2)
    cap_iota = jnp.arange(capacity, dtype=jnp.int32)
    selected = jnp.logical_and(
        (all_sources == my_group)[:, :, None], ranks[:, :, None] == cap_iota[None, None, :]
    )
    picked = jnp.sum(jnp.where(selected, all_indices[:, :, None], 0), axis=1)
    present = jnp.any(selected, axis=1)
    flat_pick = picked.reshape(-1)
    send_keys = jnp.take(nbr_keys, flat_pick, axis=0)
    send_values = jnp.take(nbr_values, flat_pick, axis=0)
    got_keys, got_values = (
        lax.all_to_all(send_keys, ("dp", "fsdp"), split_axis=0, concat_axis=0, tiled=True),
        lax.all_to_all(send_values, ("dp", "fsdp"), split_axis=0, concat_axis=0, tiled=True),
    )
    got_keys = got_keys.reshape(dp_count, fsdp_count, capacity, piece_rows, piece_width)
    got_values = got_values.reshape(dp_count, fsdp_count, capacity, piece_rows, piece_width)
    my_sources = lax.dynamic_index_in_dim(all_sources, my_place, 0, keepdims=False)
    my_ranks = lax.dynamic_index_in_dim(ranks, my_place, 0, keepdims=False)
    slot_keys = got_keys[my_sources, :, my_ranks].reshape(
        spans_here, SLOTS * neighbour_len, heads_here, HEAD_DIM
    )
    slot_values = got_values[my_sources, :, my_ranks].reshape(
        spans_here, SLOTS * neighbour_len, heads_here, HEAD_DIM
    )
    local_counts = lax.dynamic_slice_in_dim(nbr_count, my_place * spans_here, spans_here)
    live_keys = jnp.repeat(
        jnp.arange(SLOTS)[None, :] < local_counts[:, None], neighbour_len, axis=1
    )
    query_blocks = queries.reshape(spans_here, SPAN, heads_here, HEAD_DIM)
    scores = (
        jnp.einsum("cqhd,ckhd->chqk", query_blocks, slot_keys, preferred_element_type=jnp.float32)
        * scale
    )
    scores = jnp.where(live_keys[:, None, None, :], scores, -1e30)
    peak = jnp.max(scores, axis=-1, keepdims=True)
    expo = jnp.exp(scores - peak)
    probs = expo / jnp.sum(expo, axis=-1, keepdims=True)
    probs_b = probs.astype(jnp.bfloat16)
    attended = jnp.einsum(
        "chqk,ckhd->cqhd", probs_b, slot_values, preferred_element_type=jnp.float32
    )
    attended = attended.astype(jnp.bfloat16).reshape(token_rows, width_halved)
    gathered = lax.all_gather(attended, "fsdp", axis=0, tiled=True)
    upstream = lax.psum_scatter(
        lax.dot_general(
            cotangent, out_proj, (((1,), (1,)), ((), ())), preferred_element_type=jnp.float32
        ),
        "fsdp",
        scatter_dimension=0,
        tiled=True,
    ).astype(jnp.bfloat16)
    proj_term = lax.dot_general(
        gathered, cotangent, (((0,), (0,)), ((), ())), preferred_element_type=jnp.float32
    )
    grad_proj = lax.psum(proj_term.astype(jnp.bfloat16), "dp")
    upstream_blocks = upstream.reshape(spans_here, SPAN, heads_here, HEAD_DIM)
    probability_gradient = jnp.einsum(
        "cqhd,ckhd->chqk", upstream_blocks, slot_values, preferred_element_type=jnp.float32
    )
    centre = jnp.sum(probs * probability_gradient, axis=-1, keepdims=True)
    dscores = (probs * (probability_gradient - centre) * scale).astype(jnp.bfloat16)
    grad_queries = jnp.einsum(
        "chqk,ckhd->cqhd", dscores, slot_keys, preferred_element_type=jnp.float32
    )
    grad_queries = grad_queries.astype(jnp.bfloat16).reshape(token_rows, width_halved)
    slot_key_grads = jnp.einsum(
        "chqk,cqhd->ckhd", dscores, query_blocks, preferred_element_type=jnp.float32
    ).astype(jnp.bfloat16)
    value_slot_gradients = jnp.einsum(
        "chqk,cqhd->ckhd", probs_b, upstream_blocks, preferred_element_type=jnp.float32
    ).astype(jnp.bfloat16)
    location_table = jnp.logical_and(
        my_sources[None, None, :] == jnp.arange(dp_count, dtype=jnp.int32)[:, None, None],
        my_ranks[None, None, :] == cap_iota[None, :, None],
    ).astype(jnp.bfloat16)
    key_slot_table = slot_key_grads.reshape(slot_count, fsdp_count, piece_rows * piece_width)
    value_slot_table = value_slot_gradients.reshape(
        slot_count, fsdp_count, piece_rows * piece_width
    )
    back_keys = jnp.einsum(
        "vnt,tqg->vqng", location_table, key_slot_table, preferred_element_type=jnp.float32
    ).astype(jnp.bfloat16)
    back_values = jnp.einsum(
        "vnt,tqg->vqng", location_table, value_slot_table, preferred_element_type=jnp.float32
    ).astype(jnp.bfloat16)
    ret_keys, ret_values = (
        lax.all_to_all(
            back_keys.reshape(peer_count * capacity, piece_rows, piece_width),
            ("dp", "fsdp"),
            split_axis=0,
            concat_axis=0,
            tiled=True,
        ),
        lax.all_to_all(
            back_values.reshape(peer_count * capacity, piece_rows, piece_width),
            ("dp", "fsdp"),
            split_axis=0,
            concat_axis=0,
            tiled=True,
        ),
    )
    owner_table = jnp.logical_and(
        flat_pick[None, :] == jnp.arange(group_size, dtype=jnp.int32)[:, None],
        present.reshape(-1)[None, :],
    ).astype(jnp.bfloat16)
    grad_keys = jnp.dot(
        owner_table,
        ret_keys.reshape(peer_count * capacity, piece_rows * piece_width),
        preferred_element_type=jnp.float32,
    )
    grad_values = jnp.dot(
        owner_table,
        ret_values.reshape(peer_count * capacity, piece_rows * piece_width),
        preferred_element_type=jnp.float32,
    )
    grad_keys = grad_keys.astype(jnp.bfloat16).reshape(group_size, piece_rows, piece_width)
    grad_values = grad_values.astype(jnp.bfloat16).reshape(group_size, piece_rows, piece_width)
    return (attended, grad_queries, grad_keys, grad_values, grad_proj)


def solution(mesh):
    placed = (
        P(("dp", "fsdp"), "enc"),
        P("dp", "fsdp", "enc"),
        P("dp", "fsdp", "enc"),
        P("enc", "fsdp"),
        P(),
        P(),
        P(),
        P("dp", "fsdp"),
    )
    return jax.shard_map(
        local,
        mesh=mesh,
        in_specs=placed,
        out_specs=(
            P(("dp", "fsdp"), "enc"),
            P(("dp", "fsdp"), "enc"),
            P("dp", "fsdp", "enc"),
            P("dp", "fsdp", "enc"),
            P("enc", "fsdp"),
        ),
        check_vma=False,
    )
```

profile of v0, /device:TPU:1, one launch (start us, length us, event | category | flops | bytes accessed | tf_op | source)
XLA Modules:
  0.0 503.1 jit_solution(7877312089183280143)
XLA Ops:
  7.2 1.8 copy-done
  9.1 11.3 %fusion.82 = f32[1536,2048]{1,0:T(8,128)} fusion(bf16[1536,1024]{1,0:T(8,128)(2,1)S(1)} %copy-done, bf16[2048,1024]{1,0:T(8,128)(2,1)} %param.13), kind=kOutput, calls=%fused_computation.97 | convolution fusion | flops 6442450944 | bytes 19922944 | tf_op jit(solution)/shard_map/dot_general | solution.py:75
  20.4 0.6 copy-done.6
  21.0 0.1 copy.83
  21.3 0.1 convert_reduce_fusion
  21.4 0.1 copy.86
  21.6 0.1 eq.107
  21.7 0.1 copy.87
  21.8 0.1 reduce_sum.45
  22.0 0.1 reduce_sum.46
  22.1 4.7 gather_fusion.3
  26.8 4.7 gather_fusion.2
  31.5 6.4 %broadcast_select_fusion = (bf16[64,16,2048]{2,1,0:T(8,128)(2,1)}, bf16[64,16,2048]{2,1,0:T(8,128)(2,1)S(1)}) fusion(bf16[64,16,2048]{2,1,0:T(8,128)(2,1)} %gather_fusion.3, pred[64]{0:T(512)(128)(4,1)S(1)} %compare_and_fusion.1, bf16[64,16,2048]{2,1,0:T(8,128)(2,1)} %gather_fusion.2), kind=kLoop, calls=%fused_computation.14 | loop fusion | flops 4194304 | bytes 16777280 | tf_op jit(solution)/shard_map/jit(_take)/select_n | solution.py:39
  37.9 73.3 %all_to_all.20 = bf16[64,16,2048]{2,1,0:T(8,128)(2,1)} all-to-all(bf16[64,16,2048]{2,1,0:T(8,128)(2,1)S(1)} %get-tuple-element.9), channel_id=1, replica_groups=mesh['dp'=8,'fsdp'=8,'enc'=2] {'dp','fsdp'}, dimensions={0} | all-to-all | bytes 8388608 | tf_op jit(solution)/shard_map/all_to_all | solution.py:43
  111.3 10.0 %all-to-all-start.1 = ((bf16[64,16,2048]{2,1,0:T(8,128)(2,1)}), bf16[64,16,2048]{2,1,0:T(8,128)(2,1)}, u32[]{:S(2)}, u32[]{:S(2)}) async-start(bf16[64,16,2048]{2,1,0:T(8,128)(2,1)} %get-tuple-element.8), calls=%async_computation.1 | async-start | bytes 8388608 | tf_op jit(solution)/shard_map/all_to_all | solution.py:42
  121.4 0.2 dynamic-slice_reduce_fusion
  121.6 2.2 copy.105
  123.9 4.7 gather_fusion
  128.6 4.6 copy.106
  133.2 56.3 %all-to-all-done.1 = bf16[64,16,2048]{2,1,0:T(8,128)(2,1)} async-done(((bf16[64,16,2048]{2,1,0:T(8,128)(2,1)}), bf16[64,16,2048]{2,1,0:T(8,128)(2,1)}, u32[]{:S(2)}, u32[]{:S(2)}) %all-to-all-start.1) | async-done | bytes 4194336 | tf_op jit(solution)/shard_map/all_to_all | solution.py:42
  189.4 4.7 gather_fusion.1
  194.1 3.0 copy.104
  197.1 1.2 fusion.15
  198.3 0.4 copy-done.1
  198.8 1.5 fusion.81
  200.3 0.3 copy-done.2
  200.7 2.3 fusion.38
  203.0 0.5 copy.91
  203.5 1.1 copy.147
  204.6 0.2 compare_reduce_fusion
  204.9 1.7 convert_bitcast_fusion.2
  206.6 0.2 copy.108
  206.8 0.9 copy-done.5
  207.6 2.9 fusion.9
  210.5 25.1 %convert_bitcast_fusion.1 = bf16[3,256,16,128]{3,1,2,0:T(8,128)(2,1)} fusion(f32[3,16,64,256]{3,2,1,0:T(8,128)} %fusion.9, bf16[3,64,16,128]{3,2,1,0:T(8,128)(2,1)} %bitcast.119, f32[3,16,64,256]{3,2,1,0:T(8,128)} %copy-done.9, f32[3,16,64]{2,1,0:T(8,128)S(1)} %get-tuple-element.10), kind=kOutput, calls=%fused_computation.22 | convolution fusion | flops 208407808 | bytes 10235904 | tf_op jit(solution)/shard_map/chqk,cqhd->ckhd/dot_general | solution.py:96
  235.7 5.7 %copy.97 = bf16[3,256,16,128]{3,2,1,0:T(8,128)(2,1)} copy(bf16[3,256,16,128]{3,1,2,0:T(8,128)(2,1)} %convert_bitcast_fusion.1) | data formatting | bytes 6291456 | tf_op jit(solution)/shard_map/convert_element_type | solution.py:98
  241.4 6.2 %reshape.273 = bf16[6,8,32768]{2,1,0:T(8,128)(2,1)} reshape(bf16[3,256,16,128]{3,2,1,0:T(8,128)(2,1)} %copy.97) | data formatting | bytes 6291456 | tf_op jit(solution)/shard_map/reshape | solution.py:106
  247.5 3.9 fusion.2
  251.4 2.3 copy.99
  253.7 4.4 copy.110
  258.1 9.0 %all-to-all-start.2 = ((bf16[64,16,2048]{2,1,0:T(8,128)(2,1)}), bf16[64,16,2048]{2,1,0:T(8,128)(2,1)}, u32[]{:S(2)}, u32[]{:S(2)}) async-start(bf16[64,16,2048]{2,1,0:T(8,128)(2,1)} %bitcast.105), calls=%async_computation.3 | async-start | bytes 8388608 | tf_op jit(solution)/shard_map/all_to_all | solution.py:117
  267.2 5.0 convert_bitcast_fusion
  272.2 4.9 copy.101
  277.1 5.8 %reshape.277 = bf16[6,8,32768]{2,1,0:T(8,128)(2,1)} reshape(bf16[3,256,16,128]{3,2,1,0:T(8,128)(2,1)} %copy.101) | data formatting | bytes 6291456 | tf_op jit(solution)/shard_map/reshape | solution.py:107
  282.9 3.9 fusion.3
  286.8 2.3 copy.103
  289.1 4.4 copy.113
  293.5 24.8 %all-to-all-done.2 = bf16[64,16,2048]{2,1,0:T(8,128)(2,1)} async-done(((bf16[64,16,2048]{2,1,0:T(8,128)(2,1)}), bf16[64,16,2048]{2,1,0:T(8,128)(2,1)}, u32[]{:S(2)}, u32[]{:S(2)}) %all-to-all-start.2) | async-done | bytes 4194336 | tf_op jit(solution)/shard_map/all_to_all | solution.py:117
  318.2 13.6 %all-to-all-start.3 = ((bf16[64,16,2048]{2,1,0:T(8,128)(2,1)}), bf16[64,16,2048]{2,1,0:T(8,128)(2,1)}, u32[]{:S(2)}, u32[]{:S(2)}) async-start(bf16[64,16,2048]{2,1,0:T(8,128)(2,1)} %bitcast.104), calls=%async_computation.4 | async-start | bytes 8388608 | tf_op jit(solution)/shard_map/all_to_all | solution.py:124
  332.0 11.3 %convolution_convert_fusion.4 = bf16[2048,1024]{1,0:T(8,128)(2,1)} fusion(bf16[1536,2048]{1,0:T(8,128)(2,1)} %all-gather.2.cloned.1.call-done, bf16[1536,1024]{1,0:T(8,128)(2,1)S(1)} %copy-done), kind=kOutput, calls=%fused_computation.16 | convolution fusion | flops 6444548096 | bytes 13631488 | tf_op jit(solution)/shard_map/dot_general | solution.py:82
  343.3 0.1 reduce_or.14
  343.4 0.1 reduce_or.18
  343.6 23.6 %fusion.41 = bf16[3,64,16,128]{3,1,2,0:T(8,128)(2,1)} fusion(bf16[3,256,16,128]{3,2,1,0:T(8,128)(2,1)} %bitcast.112, f32[3,16,64,256]{3,2,1,0:T(8,128)} %fusion.9, f32[3,16,64,256]{3,2,1,0:T(8,128)} %copy-done.9, f32[3,16,64]{2,1,0:T(8,128)S(1)} %get-tuple-element.10), kind=kOutput, calls=%fused_computation.44 | convolution fusion | flops 207228160 | bytes 10235904 | tf_op jit(solution)/shard_map/chqk,ckhd->cqhd/dot_general | solution.py:92
  367.2 1.6 copy.95
  368.8 1.1 copy.146
  369.9 4.6 copy.111
  374.5 1.0 convolution_convert_fusion.3
  375.5 3.6 copy.112
  379.1 13.4 %all-to-all-done.3 = bf16[64,16,2048]{2,1,0:T(8,128)(2,1)} async-done(((bf16[64,16,2048]{2,1,0:T(8,128)(2,1)}), bf16[64,16,2048]{2,1,0:T(8,128)(2,1)}, u32[]{:S(2)}, u32[]{:S(2)}) %all-to-all-start.3) | async-done | bytes 4194336 | tf_op jit(solution)/shard_map/all_to_all | solution.py:124
  392.4 4.9 copy.114
  397.3 1.0 convolution_convert_fusion.2
  398.3 3.6 copy.115
  401.9 89.6 %all-reduce.2.cloned.1.call-done = bf16[2048,1024]{1,0:T(8,128)(2,1)} async-done(((bf16[2048,1024]{1,0:T(8,128)(2,1)}), bf16[2048,1024]{1,0:T(8,128)(2,1)}) %all-reduce.2.cloned.1.call-update) | async-done | bytes 4194320 | tf_op jit(solution)/shard_map/psum | solution.py:85
  491.5 4.6 copy.149
  (37 shorter events, 0.7 us)
Async XLA Ops:
  7.2 1.9 copy-start
  7.2 197.7 %reduce-scatter.2.cloned.1.call-start = ((), (), s32[]{:S(2)}) async-start(), calls=%async_computation.5 | async-start | bytes 14155776 | tf_op jit(solution)/shard_map/reduce_scatter | solution.py:74
  20.4 0.7 copy-start.6
  20.4 1.4 copy-start.7
  111.3 12.5 %copy-start.8 = (s32[192]{0:T(256)S(1)}, s32[192]{0:T(256)}, u32[]{:S(2)}) copy-start(s32[192]{0:T(256)} %param.16) | copy-start | bytes 2308
  111.3 78.2 %all-to-all-start.1 = ((bf16[64,16,2048]{2,1,0:T(8,128)(2,1)}), bf16[64,16,2048]{2,1,0:T(8,128)(2,1)}, u32[]{:S(2)}, u32[]{:S(2)}) async-start(bf16[64,16,2048]{2,1,0:T(8,128)(2,1)} %get-tuple-element.8), calls=%async_computation.1 | async-start | bytes 8388608 | tf_op jit(solution)/shard_map/all_to_all | solution.py:42
  121.3 210.6 %all-gather.2.cloned.1.call-start = ((), (), s32[]{:S(2)}) async-start(), calls=%async_computation.6 | async-start | bytes 7077888 | tf_op jit(solution)/shard_map/all_gather | solution.py:73
  194.1 3.0 copy-start.4
  197.1 1.7 copy-start.1
  198.8 1.9 copy-start.2
  200.3 2.7 copy-start.9
  204.9 2.8 copy-start.3
  206.8 0.9 copy-start.5
  258.1 60.1 %all-to-all-start.2 = ((bf16[64,16,2048]{2,1,0:T(8,128)(2,1)}), bf16[64,16,2048]{2,1,0:T(8,128)(2,1)}, u32[]{:S(2)}, u32[]{:S(2)}) async-start(bf16[64,16,2048]{2,1,0:T(8,128)(2,1)} %bitcast.105), calls=%async_computation.3 | async-start | bytes 8388608 | tf_op jit(solution)/shard_map/all_to_all | solution.py:117
  318.2 74.2 %all-to-all-start.3 = ((bf16[64,16,2048]{2,1,0:T(8,128)(2,1)}), bf16[64,16,2048]{2,1,0:T(8,128)(2,1)}, u32[]{:S(2)}, u32[]{:S(2)}) async-start(bf16[64,16,2048]{2,1,0:T(8,128)(2,1)} %bitcast.104), calls=%async_computation.4 | async-start | bytes 8388608 | tf_op jit(solution)/shard_map/all_to_all | solution.py:124
  331.9 159.6 %all-reduce.2.cloned.1.call-start = ((), (), s32[]{:S(2)}) async-start(), calls=%async_computation.7 | async-start | bytes 8388608 | tf_op jit(solution)/shard_map/psum | solution.py:85
Sparse Core Ops, SparseCore 0:
  20.5 164.9 reduce-scatter.1
  204.8 41.3 all-gather.1
  343.4 148.0 all-reduce.1
where the time goes:
time: 511 us; the launch traced here: 503 us
  waiting for transfers between devices  184 us (36%)
  local copies, waits for them, and re-layouts  95.6 us (19%)
  matrix products  92.5 us (18%)
  blocking collectives  73.3 us (14%)
  starting transfers between devices  32.8 us (6%)
  between operations  14.5 us (3%)
  other arithmetic  10.3 us (2%)
    psum x1, waiting for transfers between devices, local(): grad_proj = lax.psum(proj_term.astype(jnp.bfloat16), 'dp')  89.6 us
    all_to_all x1, blocking collectives, local(): lax.all_to_all(send_values, ('dp', 'fsdp'), split_axis=0, concat_axis=0,...  73.3 us
    all_to_all x1, waiting for transfers between devices, local(): lax.all_to_all(send_keys, ('dp', 'fsdp'), split_axis=0, concat_axis=0, ti...  56.3 us
    unnamed x34, local copies, waits for them, and re-layouts  46.4 us
    dot_general x1, matrix products, local(): jnp.einsum('chqk,cqhd->ckhd', dscores, query_blocks, preferred_element_ty...  25.1 us
    all_to_all x1, waiting for transfers between devices, local(): lax.all_to_all(back_keys.reshape(peer_count * capacity, piece_rows, piece...  24.8 us
    dot_general x1, matrix products, local(): jnp.einsum('chqk,ckhd->cqhd', dscores, slot_keys, preferred_element_type=...  23.6 us
    all_to_all x1, starting transfers between devices, local(): lax.all_to_all(back_values.reshape(peer_count * capacity, piece_rows, pie...  13.6 us
  transfers between devices with their start and end apart: 6, of which 4 were waited for; matrix products, arithmetic and copies ran while one was open for 35% of the time, Pallas kernels for 0%

commit v1 on v0

--- a/solution.py
+++ b/solution.py
@@ -82,7 +82,9 @@
     proj_term = lax.dot_general(
         gathered, cotangent, (((0,), (0,)), ((), ())), preferred_element_type=jnp.float32
     )
-    grad_proj = lax.psum(proj_term.astype(jnp.bfloat16), "dp")
+    x = proj_term.astype(jnp.bfloat16)
+    pieces = lax.all_gather(x, "dp", axis=0, tiled=False)
+    grad_proj = pieces.sum(axis=0)
     upstream_blocks = upstream.reshape(spans_here, SPAN, heads_here, HEAD_DIM)
     probability_gradient = jnp.einsum(
         "cqhd,ckhd->chqk", upstream_blocks, slot_values, preferred_element_type=jnp.float32

time: 511 us -> 740 us (1.45)
  waiting for transfers between devices: 184 us -> 438 us
  other arithmetic: 10.3 us -> 24.6 us
  local copies, waits for them, and re-layouts: 95.6 us -> 82.4 us
  blocking collectives: 73.3 us -> 63.9 us
  starting transfers between devices: 32.8 us -> 23.8 us
  matrix products: 92.5 us -> 84.4 us
    all_gather x0 -> x1, waiting for transfers between devices: none -> 238 us  [local(): pieces = lax.all_gather(x, 'dp', axis=0, tiled=False)]
    psum x1 -> x0, waiting for transfers between devices: 89.6 us -> none  [local(): grad_proj = lax.psum(proj_term.astype(jnp.bfloat16), 'dp')]
    reduce_scatter x1, waiting for transfers between devices: 0.02 us -> 62.5 us  [local(): lax.psum_scatter(lax.dot_general(cotangent, out_proj, (((1,), (1,)), ((),...]
    all_gather x1, waiting for transfers between devices: 0.02 us -> 40.7 us  [local(): gathered = lax.all_gather(attended, 'fsdp', axis=0, tiled=True)]
    all_to_all x1, waiting for transfers between devices: 13.4 us -> 34.3 us  [local(): lax.all_to_all(back_values.reshape(peer_count * capacity, piece_rows, pie...]
    all_to_all x1, waiting for transfers between devices: 56.3 us -> 39.3 us  [local(): lax.all_to_all(send_values, ('dp', 'fsdp'), split_axis=0, concat_axis=0,...]
    reduce_sum x0 -> x1, other arithmetic: none -> 14.5 us  [local(): grad_proj = pieces.sum(axis=0)]
    all_to_all x1, blocking collectives: 73.3 us -> 63.9 us  [local(): lax.all_to_all(send_keys, ('dp', 'fsdp'), split_axis=0, concat_axis=0, ti...]
  transfers between devices with their start and end apart: 6 -> 6, of which waited for: 4 -> 6; matrix products, arithmetic and copies ran while one was open for 35% -> 20% of each run, Pallas kernels for 0% -> 0%
where the time goes in v1:
time: 740 us; the launch traced here: 731 us
  waiting for transfers between devices  438 us (59%)
  matrix products  84.4 us (11%)
  local copies, waits for them, and re-layouts  82.4 us (11%)
  blocking collectives  63.9 us (9%)
  other arithmetic  24.6 us (3%)
  starting transfers between devices  23.8 us (3%)
  between operations  14.3 us (2%)
    all_gather x1, waiting for transfers between devices, local(): pieces = lax.all_gather(x, 'dp', axis=0, tiled=False)  238 us
    all_to_all x1, blocking collectives, local(): lax.all_to_all(send_keys, ('dp', 'fsdp'), split_axis=0, concat_axis=0, ti...  63.9 us
    reduce_scatter x1, waiting for transfers between devices, local(): lax.psum_scatter(lax.dot_general(cotangent, out_proj, (((1,), (1,)), ((),...  62.5 us
    all_gather x1, waiting for transfers between devices, local(): gathered = lax.all_gather(attended, 'fsdp', axis=0, tiled=True)  40.7 us
    all_to_all x1, waiting for transfers between devices, local(): lax.all_to_all(send_values, ('dp', 'fsdp'), split_axis=0, concat_axis=0,...  39.3 us
    unnamed x33, local copies, waits for them, and re-layouts  38.2 us
    all_to_all x1, waiting for transfers between devices, local(): lax.all_to_all(back_values.reshape(peer_count * capacity, piece_rows, pie...  34.3 us
    all_to_all x1, waiting for transfers between devices, local(): lax.all_to_all(back_keys.reshape(peer_count * capacity, piece_rows, piece...  23.3 us
  transfers between devices with their start and end apart: 6, of which 6 were waited for; matrix products, arithmetic and copies ran while one was open for 20% of the time, Pallas kernels for 0%

profile of v1, /device:TPU:1, one launch (start us, length us, event | category | flops | bytes accessed | tf_op | source)
XLA Modules:
  0.0 731.3 jit_solution(3055345593283386107)
XLA Ops:
  7.2 0.9 copy.83
  8.3 0.1 convert_reduce_fusion
  8.4 0.1 copy.86
  8.6 0.1 eq.107
  8.7 0.1 copy.87
  8.8 0.7 fusion.80
  9.5 0.7 select_reduce_fusion
  10.2 0.1 reduce_sum.57
  10.3 0.1 reduce_sum.58
  10.5 4.6 gather_fusion.2
  15.1 4.7 gather_fusion.3
  19.8 5.2 broadcast_select_fusion
  25.1 63.9 %all_to_all.20 = bf16[64,16,2048]{2,1,0:T(8,128)(2,1)} all-to-all(bf16[64,16,2048]{2,1,0:T(8,128)(2,1)S(1)} %get-tuple-element.8), channel_id=1, replica_groups=mesh['dp'=8,'fsdp'=8,'enc'=2] {'dp','fsdp'}, dimensions={0} | all-to-all | bytes 8388608 | tf_op jit(solution)/shard_map/all_to_all | solution.py:42
  88.9 7.3 all-to-all-start
  96.3 0.2 dynamic-slice_reduce_fusion
  96.5 2.2 copy.105
  98.8 4.7 gather_fusion.1
  103.5 4.6 copy.104
  108.1 39.3 %all-to-all-done = bf16[64,16,2048]{2,1,0:T(8,128)(2,1)} async-done(((bf16[64,16,2048]{2,1,0:T(8,128)(2,1)}), bf16[64,16,2048]{2,1,0:T(8,128)(2,1)}, u32[]{:S(2)}, u32[]{:S(2)}) %all-to-all-start) | async-done | bytes 4194336 | tf_op jit(solution)/shard_map/all_to_all | solution.py:43
  147.4 4.7 gather_fusion
  152.0 3.1 copy.106
  155.1 1.2 fusion.15
  156.4 1.3 fusion.81
  157.7 2.4 fusion.38
  160.1 0.5 copy.91
  160.6 1.1 copy.147
  161.8 11.3 %fusion.82 = f32[1536,2048]{1,0:T(8,128)} fusion(bf16[1536,1024]{1,0:T(8,128)(2,1)S(1)} %copy-done, bf16[2048,1024]{1,0:T(8,128)(2,1)} %param.13), kind=kOutput, calls=%fused_computation.97 | convolution fusion | flops 6442450944 | bytes 19922944 | tf_op jit(solution)/shard_map/dot_general | solution.py:75
  173.1 0.2 all-gather.6.cloned.1.call-start
  173.3 40.7 %all-gather.4.cloned.1.call-done = bf16[1536,2048]{1,0:T(8,128)(2,1)} async-done(((bf16[192,2048]{1,0:T(8,128)(2,1)}), bf16[1536,2048]{1,0:T(8,128)(2,1)}) %all-gather.4.cloned.1.call-update) | async-done | bytes 6291472 | tf_op jit(solution)/shard_map/all_gather | solution.py:73
  214.0 11.2 %convolution_convert_fusion.4 = bf16[2048,1024]{1,0:T(8,128)(2,1)} fusion(bf16[1536,2048]{1,0:T(8,128)(2,1)} %all-gather.4.cloned.1.call-done, bf16[1536,1024]{1,0:T(8,128)(2,1)S(1)} %copy-done), kind=kOutput, calls=%fused_computation.16 | convolution fusion | flops 6444548096 | bytes 13631488 | tf_op jit(solution)/shard_map/dot_general | solution.py:82
  225.2 0.2 compare_reduce_fusion
  225.4 62.5 %reduce-scatter.2.cloned.1.call-done = f32[192,2048]{1,0:T(8,128)} async-done(((f32[1536,2048]{1,0:T(8,128)}), f32[192,2048]{1,0:T(8,128)}) %reduce-scatter.2.cloned.1.call-update) | async-done | bytes 1572880 | tf_op jit(solution)/shard_map/reduce_scatter | solution.py:74
  287.9 1.5 convert_bitcast_fusion.2
  289.5 0.2 copy.108
  289.7 5.0 convert_bitcast_fusion
  294.7 4.9 copy.101
  299.6 4.5 reshape.277
  304.1 2.0 fusion.3
  306.1 2.3 copy.103
  308.4 4.3 copy.113
  312.7 10.1 %all-to-all-start.3 = ((bf16[64,16,2048]{2,1,0:T(8,128)(2,1)}), bf16[64,16,2048]{2,1,0:T(8,128)(2,1)}, u32[]{:S(2)}, u32[]{:S(2)}) async-start(bf16[64,16,2048]{2,1,0:T(8,128)(2,1)} %bitcast.107), calls=%async_computation.4 | async-start | bytes 8388608 | tf_op jit(solution)/shard_map/all_to_all | solution.py:126
  322.9 4.0 fusion.9
  326.9 23.1 %convert_bitcast_fusion.1 = bf16[3,256,16,128]{3,1,2,0:T(8,128)(2,1)S(1)} fusion(f32[3,16,64,256]{3,2,1,0:T(8,128)} %fusion.9, bf16[3,64,16,128]{3,2,1,0:T(8,128)(2,1)} %bitcast.121, f32[3,16,64,256]{3,2,1,0:T(8,128)} %copy-done.9, f32[3,16,64]{2,1,0:T(8,128)S(1)} %get-tuple-element.10), kind=kOutput, calls=%fused_computation.22 | convolution fusion | flops 208407808 | bytes 10235904 | tf_op jit(solution)/shard_map/chqk,cqhd->ckhd/dot_general | solution.py:98
  350.0 3.7 copy.97
  353.7 4.5 reshape.273
  358.2 2.0 fusion.2
  360.2 2.3 copy.99
  362.5 4.4 copy.110
  366.9 34.3 %all-to-all-done.3 = bf16[64,16,2048]{2,1,0:T(8,128)(2,1)} async-done(((bf16[64,16,2048]{2,1,0:T(8,128)(2,1)}), bf16[64,16,2048]{2,1,0:T(8,128)(2,1)}, u32[]{:S(2)}, u32[]{:S(2)}) %all-to-all-start.3) | async-done | bytes 4194336 | tf_op jit(solution)/shard_map/all_to_all | solution.py:126
  401.2 6.1 all-to-all-start.2
  407.3 0.1 reduce_or.14
  407.5 0.1 reduce_or.18
  407.6 20.4 %fusion.41 = bf16[3,64,16,128]{3,1,2,0:T(8,128)(2,1)} fusion(bf16[3,256,16,128]{3,2,1,0:T(8,128)(2,1)S(1)} %bitcast.114, f32[3,16,64,256]{3,2,1,0:T(8,128)} %fusion.9, f32[3,16,64,256]{3,2,1,0:T(8,128)} %copy-done.9, f32[3,16,64]{2,1,0:T(8,128)S(1)} %get-tuple-element.10), kind=kOutput, calls=%fused_computation.44 | convolution fusion | flops 207228160 | bytes 10235904 | tf_op jit(solution)/shard_map/chqk,ckhd->cqhd/dot_general | solution.py:94
  428.0 1.6 copy.95
  429.6 1.1 copy.146
  430.7 4.6 copy.114
  435.3 1.0 convolution_convert_fusion.2
  436.3 3.6 copy.115
  439.9 23.3 %all-to-all-done.2 = bf16[64,16,2048]{2,1,0:T(8,128)(2,1)} async-done(((bf16[64,16,2048]{2,1,0:T(8,128)(2,1)}), bf16[64,16,2048]{2,1,0:T(8,128)(2,1)}, u32[]{:S(2)}, u32[]{:S(2)}) %all-to-all-start.2) | async-done | bytes 4194336 | tf_op jit(solution)/shard_map/all_to_all | solution.py:119
  463.1 4.6 copy.111
  467.7 1.0 convolution_convert_fusion.3
  468.7 3.6 copy.112
  472.3 237.9 %all-gather.6.cloned.1.call-done = bf16[16384,1024]{1,0:T(8,128)(2,1)} async-done(((bf16[2048,1024]{1,0:T(8,128)(2,1)}), bf16[16384,1024]{1,0:T(8,128)(2,1)}) %all-gather.6.cloned.1.call-update) | async-done | bytes 33554448 | tf_op jit(solution)/shard_map/all_gather | solution.py:86
  710.2 14.5 %reduce_sum.61 = bf16[2048,1024]{1,0:T(8,128)(2,1)} reduce(bf16[8,2048,1024]{2,1,0:T(8,128)(2,1)} %bitcast.105, bf16[]{:T(256)} %constant.52.clone.1), dimensions={0}, to_apply=%region_9.11 | reduce | flops 14680064 | bytes 37748736 | tf_op jit(solution)/shard_map/reduce_sum | solution.py:87
  (37 shorter events, 0.5 us)
Async XLA Ops:
  7.2 154.6 %copy-start = (bf16[1536,1024]{1,0:T(8,128)(2,1)S(1)}, bf16[1536,1024]{1,0:T(8,128)(2,1)}, u32[]{:S(2)}) copy-start(bf16[1536,1024]{1,0:T(8,128)(2,1)} %param.17) | copy-start | bytes 9437188
  88.9 9.7 %copy-start.8 = (s32[192]{0:T(256)S(1)}, s32[192]{0:T(256)}, u32[]{:S(2)}) copy-start(s32[192]{0:T(256)} %param.16) | copy-start | bytes 2308
  88.9 58.4 %all-to-all-start = ((bf16[64,16,2048]{2,1,0:T(8,128)(2,1)}), bf16[64,16,2048]{2,1,0:T(8,128)(2,1)}, u32[]{:S(2)}, u32[]{:S(2)}) async-start(bf16[64,16,2048]{2,1,0:T(8,128)(2,1)} %get-tuple-element.9), calls=%async_computation | async-start | bytes 8388608 | tf_op jit(solution)/shard_map/all_to_all | solution.py:43
  96.2 117.8 %all-gather.4.cloned.1.call-start = ((), (), s32[]{:S(2)}) async-start(), calls=%async_computation.6 | async-start | bytes 7077888 | tf_op jit(solution)/shard_map/all_gather | solution.py:73
  152.0 3.1 copy-start.2
  152.0 3.1 copy-start.6
  155.1 2.6 copy-start.4
  157.7 2.4 copy-start.9
  161.7 126.2 %reduce-scatter.2.cloned.1.call-start = ((), (), s32[]{:S(2)}) async-start(), calls=%async_computation.5 | async-start | bytes 14155776 | tf_op jit(solution)/shard_map/reduce_scatter | solution.py:74
  173.1 537.1 %all-gather.6.cloned.1.call-start = ((), (), s32[]{:S(2)}) async-start(), calls=%async_computation.7 | async-start | bytes 37748736 | tf_op jit(solution)/shard_map/all_gather | solution.py:86
  289.7 5.0 copy-start.7
  312.7 10.2 %copy-start.5 = (bf16[96,8,16,128]{3,2,1,0:T(8,128)(2,1)S(1)}, bf16[96,8,16,128]{3,2,1,0:T(8,128)(2,1)}, u32[]{:S(2)}) copy-start(bf16[96,8,16,128]{3,2,1,0:T(8,128)(2,1)} %copy-done.4) | copy-start | bytes 9437188
  312.7 88.5 %all-to-all-start.3 = ((bf16[64,16,2048]{2,1,0:T(8,128)(2,1)}), bf16[64,16,2048]{2,1,0:T(8,128)(2,1)}, u32[]{:S(2)}, u32[]{:S(2)}) async-start(bf16[64,16,2048]{2,1,0:T(8,128)(2,1)} %bitcast.107), calls=%async_computation.4 | async-start | bytes 8388608 | tf_op jit(solution)/shard_map/all_to_all | solution.py:126
  401.2 6.3 copy-start.3
  401.2 61.9 %all-to-all-start.2 = ((bf16[64,16,2048]{2,1,0:T(8,128)(2,1)}), bf16[64,16,2048]{2,1,0:T(8,128)(2,1)}, u32[]{:S(2)}, u32[]{:S(2)}) async-start(bf16[64,16,2048]{2,1,0:T(8,128)(2,1)} %bitcast.106), calls=%async_computation.3 | async-start | bytes 8388608 | tf_op jit(solution)/shard_map/all_to_all | solution.py:119
  710.2 14.5 %copy-start.1 = (bf16[1536,1024]{1,0:T(8,128)(2,1)S(1)}, bf16[1536,1024]{1,0:T(8,128)(2,1)}, u32[]{:S(2)}) copy-start(bf16[1536,1024]{1,0:T(8,128)(2,1)} %param.17) | copy-start | bytes 9437188
Sparse Core Ops, SparseCore 0:
  161.9 52.0 all-gather.3
  216.4 71.4 reduce-scatter.1
  290.3 419.8 all-gather.5
